TPU v7x, 32 devices: a whole 2x2x4 slice. The times are simulated.
32 devices in a mesh: gy: 8 (over y, x, core), gz: 4 (over z).
Axes of the slice: x: 2, y: 2, z: 4, core: 2. Of those that a mesh axis runs over, the one named last changes fastest.
Arguments:
- fuel: float32 [128, 16, 2048], P('gy', 'gz'), may hold values from -6 to 6
- oxidant: float32 [128, 16, 2048], P('gy', 'gz'), may hold values from -6 to 6
- rate: float32 [128, 16, 2048], P('gy', 'gz'), may hold values from 0.05 to 0.5
- velocity: float32 [3], replicated, may hold values from -0.3 to 0.3
- sketch_x: float32 [128, 2048], replicated, may hold values from -0.125 to 0.125
- sketch_y: float32 [128, 128], replicated, may hold values from -0.5 to 0.5
Outputs:
- sketch: float32 [128, 2, 16, 128], P('gy', None, 'gz')
All inputs are finite; a program needn't handle non-finite values.
Results may differ from a plain program's by a relative error of at most 0.00014.
Values sent between devices are 32-bit elements; how exact they have to be, the bound alone decides.
No kernel may reach another device: no remote copies, remote signals or barrier semaphores. Data moves between devices by JAX's collectives and lax.ppermute only.
A program may use at most 64 MiB of HBM per device.

v0:
```python
import jax
import jax.numpy as jnp
from jax import lax
from jax.sharding import PartitionSpec as P

STEPS = 2


def extended(cells, sides, width):
    for axis, dim in sides:
        count = lax.axis_size(axis)
        ends = count - 1
        head = lax.slice_in_dim(cells, 0, width, axis=dim)
        tail = lax.slice_in_dim(cells, cells.shape[dim] - width, cells.shape[dim], axis=dim)
        cells = jnp.concatenate(
            [
                lax.ppermute(tail, axis, [(i, (i + 1) % count) for i in range(ends)]),
                cells,
                lax.ppermute(head, axis, [((i + 1) % count, i) for i in range(ends)]),
            ],
            axis=dim,
        )
    return cells


def advance(padded, rate, velocity):
    core = padded[:, 1:-1, 1:-1, :]
    xpad = jnp.pad(core, ((0, 0), (0, 0), (0, 0), (1, 1)))
    east = xpad[..., 2:]
    west = xpad[..., :-2]
    north = padded[:, 2:, 1:-1, :]
    south = padded[:, :-2, 1:-1, :]
    upper = padded[:, 1:-1, 2:, :]
    lower = padded[:, 1:-1, :-2, :]
    lap = east + west + north + south + upper + lower - 6.0 * core
    adv = 0.5 * (
        velocity[0] * (east - west) + velocity[1] * (north - south) + velocity[2] * (upper - lower)
    )
    react = rate * core[0] * core[1]
    new_fuel = core[0] + 0.1 * lap[0] - adv[0] - react
    new_oxid = core[1] + 0.05 * lap[1] - adv[1] + react
    return jnp.stack([new_fuel, new_oxid])


def per_device(fuel, oxidant, rate, velocity, sketch_x, sketch_y):
    rows_local = fuel.shape[0]
    planes_local = fuel.shape[1]
    width_x = fuel.shape[2]
    fields = jnp.stack([fuel, oxidant])
    for step in range(STEPS):
        padded = extended(fields, (("gy", 1), ("gz", 2)), 1)
        fields = advance(padded, rate, velocity)
    flat = fields.reshape(-1, width_x)
    projected = lax.dot_general(
        sketch_x, flat, (((1,), (1,)), ((), ())), precision=lax.Precision.HIGHEST
    )
    projected = projected.reshape(sketch_x.shape[0], 2, rows_local, planes_local)
    moved = lax.all_to_all(projected, "gy", split_axis=0, concat_axis=2, tiled=True)
    return jnp.einsum("kfyz,jy->kfzj", moved, sketch_y, precision=lax.Precision.HIGHEST)


def solution(mesh):
    in_specs = (P("gy", "gz", None), P("gy", "gz", None), P("gy", "gz", None), P(), P(), P())
    out_specs = P("gy", None, "gz", None)
    return jax.shard_map(
        per_device, mesh=mesh, in_specs=in_specs, out_specs=out_specs, check_vma=False
    )
```

profile of v0, /device:TPU:0, one launch (start us, length us, event | category | flops | bytes accessed | tf_op | source)
XLA Modules:
  0.0 70.9 jit_solution(7540009684919437268)
XLA Ops:
  0.0 1.0 %fusion.21 = (f32[2,1,4,2048]{3,2,1,0:T(4,128)S(1)}, f32[2,1,4,2048]{3,2,1,0:T(4,128)S(1)}) fusion(f32[1,16,4,2048]{3,2,1,0:T(4,128)} %bitcast.99, f32[1,16,4,2048]{3,2,1,0:T(4,128)} %bitcast.94), kind=kLoop, calls=%fused_computation.83 | loop fusion | flops 32768 | bytes 1179648 | tf_op jit(solution)/shard_map/stack | solution.py:49
  1.0 1.3 %collective-permute-start = (f32[2,1,4,2048]{3,2,1,0:T(4,128)S(1)}, f32[2,1,4,2048]{3,2,1,0:T(4,128)S(1)}, u32[]{:S(2)}, u32[]{:S(2)}) collective-permute-start(f32[2,1,4,2048]{3,2,1,0:T(4,128)S(1)} %get-tuple-element.16), channel_id=1, source_target_pairs={{4,0},{8,4},{12,8},{16,12},{20,16},{24,20},{28,24},{5,1},{9,5},{13... | collective-permute-start | bytes 196616 | tf_op jit(solution)/shard_map/ppermute | solution.py:19
  2.3 3.0 %collective-permute-start.1 = (f32[2,1,4,2048]{3,2,1,0:T(4,128)S(1)}, f32[2,1,4,2048]{3,2,1,0:T(4,128)S(1)}, u32[]{:S(2)}, u32[]{:S(2)}) collective-permute-start(f32[2,1,4,2048]{3,2,1,0:T(4,128)S(1)} %get-tuple-element.15), channel_id=1, source_target_pairs={{0,4},{4,8},{8,12},{12,16},{16,20},{20,24},{24,28},{1,5},{5,9},{9,... | collective-permute-start | bytes 196616 | tf_op jit(solution)/shard_map/ppermute | solution.py:17
  5.4 0.9 %collective-permute-done.1 = f32[2,1,4,2048]{3,2,1,0:T(4,128)S(1)} collective-permute-done((f32[2,1,4,2048]{3,2,1,0:T(4,128)S(1)}, f32[2,1,4,2048]{3,2,1,0:T(4,128)S(1)}, u32[]{:S(2)}, u32[]{:S(2)}) %collective-permute-start.1) | collective-permute-done | bytes 65568 | tf_op jit(solution)/shard_map/ppermute | solution.py:17
  6.7 1.3 %collective-permute-start.2 = (f32[2,18,1,2048]{3,2,1,0:T(1,128)S(1)}, f32[2,18,1,2048]{3,2,1,0:T(1,128)S(1)}, u32[]{:S(2)}, u32[]{:S(2)}) collective-permute-start(f32[2,18,1,2048]{3,2,1,0:T(1,128)S(1)} %get-tuple-element.12), channel_id=1, source_target_pairs={{1,0},{2,1},{3,2},{5,4},{6,5},{7,6},{9,8},{10,9},{11,10},{13,12},{... | collective-permute-start | bytes 884744 | tf_op jit(solution)/shard_map/ppermute | solution.py:19
  8.0 5.6 %collective-permute-start.3 = (f32[2,18,1,2048]{3,2,1,0:T(1,128)S(1)}, f32[2,18,1,2048]{3,2,1,0:T(1,128)S(1)}, u32[]{:S(2)}, u32[]{:S(2)}) collective-permute-start(f32[2,18,1,2048]{3,2,1,0:T(1,128)S(1)} %get-tuple-element.11), channel_id=1, source_target_pairs={{0,1},{1,2},{2,3},{4,5},{5,6},{6,7},{8,9},{9,10},{10,11},{12,13},{... | collective-permute-start | bytes 884744 | tf_op jit(solution)/shard_map/ppermute | solution.py:17
  14.7 3.8 %collective-permute-done.2 = f32[2,18,1,2048]{3,2,1,0:T(1,128)S(1)} collective-permute-done((f32[2,18,1,2048]{3,2,1,0:T(1,128)S(1)}, f32[2,18,1,2048]{3,2,1,0:T(1,128)S(1)}, u32[]{:S(2)}, u32[]{:S(2)}) %collective-permute-start.2) | collective-permute-done | bytes 294944 | tf_op jit(solution)/shard_map/ppermute | solution.py:19
  18.5 1.7 %collective-permute-done.3 = f32[2,18,1,2048]{3,2,1,0:T(1,128)S(1)} collective-permute-done((f32[2,18,1,2048]{3,2,1,0:T(1,128)S(1)}, f32[2,18,1,2048]{3,2,1,0:T(1,128)S(1)}, u32[]{:S(2)}, u32[]{:S(2)}) %collective-permute-start.3) | collective-permute-done | bytes 294944 | tf_op jit(solution)/shard_map/ppermute | solution.py:17
  20.2 2.3 %multiply_subtract_fusion.1 = f32[2,16,4,2048]{3,2,1,0:T(4,128)S(1)} fusion(f32[2,16,4,2048]{3,2,1,0:T(4,128)S(1)} %pad_maximum_fusion, f32[2,1,4,2048]{3,2,1,0:T(4,128)S(1)} %collective-permute-done, f32[1,16,4,2048]{3,2,1,0:T(4,128)S(1)} %bitcast.97, f32[1,16,4,2048]{3,2,1,0:T(4,128)S(1)} %bitcast.102, f32[2,1,4,2048]{3,2,1,0:T(4,128)S(1)} %collective-permute-done.1, ...), kind=kLoop, calls=%fused_computation.38 | loop fusion | flops 4980736 | bytes 3866624 | tf_op jit(solution)/shard_map/sub | solution.py:35
  22.5 4.4 %add_multiply_fusion.1 = f32[2,16,4,2048]{3,2,1,0:T(4,128)S(1)} fusion(f32[2,16,4,2048]{3,2,1,0:T(4,128)S(1)} %pad_maximum_fusion, f32[]{:T(128)} %bitcast.5, f32[]{:T(128)} %bitcast.4, f32[]{:T(128)} %bitcast.3, f32[2,1,4,2048]{3,2,1,0:T(4,128)S(1)} %collective-permute-done, f32[1,16,4,2048]{3,2,1,0:T(4,128)S(1)} %bitcast.98, ...), kind=kLoop, calls=%fused_computation.37 | loop fusion | flops 5505024 | bytes 3866636 | tf_op jit(solution)/shard_map/mul | solution.py:36
  26.9 1.0 %fusion.15 = (f32[16,4,2048]{2,1,0:T(4,128)S(1)}, f32[16,4,2048]{2,1,0:T(4,128)S(1)}) fusion(f32[2,16,4,2048]{3,2,1,0:T(4,128)S(1)} %add_multiply_fusion.1, f32[16,4,2048]{2,1,0:T(4,128)S(1)} %copy-done.2, f32[2,16,4,2048]{3,2,1,0:T(4,128)S(1)} %multiply_subtract_fusion.1, f32[16,4,2048]{2,1,0:T(4,128)S(1)} %copy-done.1, f32[16,4,2048]{2,1,0:T(4,128)S(1)} %copy-done.3), kind=kLoop, calls=%fused_computation.65 | loop fusion | flops 1310720 | bytes 4718592 | tf_op jit(solution)/shard_map/sub | solution.py:40
  27.9 1.3 %collective-permute-start.4 = (f32[2,1,4,2048]{3,2,1,0:T(4,128)S(1)}, f32[2,1,4,2048]{3,2,1,0:T(4,128)S(1)}, u32[]{:S(2)}, u32[]{:S(2)}) collective-permute-start(f32[2,1,4,2048]{3,2,1,0:T(4,128)S(1)} %get-tuple-element.14), channel_id=1, source_target_pairs={{4,0},{8,4},{12,8},{16,12},{20,16},{24,20},{28,24},{5,1},{9,5},{13... | collective-permute-start | bytes 196616 | tf_op jit(solution)/shard_map/ppermute | solution.py:19
  29.2 3.4 %collective-permute-start.5 = (f32[2,1,4,2048]{3,2,1,0:T(4,128)S(1)}, f32[2,1,4,2048]{3,2,1,0:T(4,128)S(1)}, u32[]{:S(2)}, u32[]{:S(2)}) collective-permute-start(f32[2,1,4,2048]{3,2,1,0:T(4,128)S(1)} %get-tuple-element.13), channel_id=1, source_target_pairs={{0,4},{4,8},{8,12},{12,16},{16,20},{20,24},{24,28},{1,5},{5,9},{9,... | collective-permute-start | bytes 196616 | tf_op jit(solution)/shard_map/ppermute | solution.py:17
  32.6 0.9 %collective-permute-done.5 = f32[2,1,4,2048]{3,2,1,0:T(4,128)S(1)} collective-permute-done((f32[2,1,4,2048]{3,2,1,0:T(4,128)S(1)}, f32[2,1,4,2048]{3,2,1,0:T(4,128)S(1)}, u32[]{:S(2)}, u32[]{:S(2)}) %collective-permute-start.5) | collective-permute-done | bytes 65568 | tf_op jit(solution)/shard_map/ppermute | solution.py:17
  34.0 1.3 %collective-permute-start.6 = (f32[2,18,1,2048]{3,2,1,0:T(1,128)S(1)}, f32[2,18,1,2048]{3,2,1,0:T(1,128)S(1)}, u32[]{:S(2)}, u32[]{:S(2)}) collective-permute-start(f32[2,18,1,2048]{3,2,1,0:T(1,128)S(1)} %get-tuple-element.10), channel_id=1, source_target_pairs={{1,0},{2,1},{3,2},{5,4},{6,5},{7,6},{9,8},{10,9},{11,10},{13,12},{... | collective-permute-start | bytes 884744 | tf_op jit(solution)/shard_map/ppermute | solution.py:19
  35.3 4.7 %collective-permute-start.7 = (f32[2,18,1,2048]{3,2,1,0:T(1,128)S(1)}, f32[2,18,1,2048]{3,2,1,0:T(1,128)S(1)}, u32[]{:S(2)}, u32[]{:S(2)}) collective-permute-start(f32[2,18,1,2048]{3,2,1,0:T(1,128)S(1)} %get-tuple-element.9), channel_id=1, source_target_pairs={{0,1},{1,2},{2,3},{4,5},{5,6},{6,7},{8,9},{9,10},{10,11},{12,13},{... | collective-permute-start | bytes 884744 | tf_op jit(solution)/shard_map/ppermute | solution.py:17
  40.4 2.4 %collective-permute-done.6 = f32[2,18,1,2048]{3,2,1,0:T(1,128)S(1)} collective-permute-done((f32[2,18,1,2048]{3,2,1,0:T(1,128)S(1)}, f32[2,18,1,2048]{3,2,1,0:T(1,128)S(1)}, u32[]{:S(2)}, u32[]{:S(2)}) %collective-permute-start.6) | collective-permute-done | bytes 294944 | tf_op jit(solution)/shard_map/ppermute | solution.py:19
  42.8 1.7 %collective-permute-done.7 = f32[2,18,1,2048]{3,2,1,0:T(1,128)S(1)} collective-permute-done((f32[2,18,1,2048]{3,2,1,0:T(1,128)S(1)}, f32[2,18,1,2048]{3,2,1,0:T(1,128)S(1)}, u32[]{:S(2)}, u32[]{:S(2)}) %collective-permute-start.7) | collective-permute-done | bytes 294944 | tf_op jit(solution)/shard_map/ppermute | solution.py:17
  44.6 4.3 %add_multiply_fusion = f32[2,16,4,2048]{3,2,1,0:T(4,128)S(1)} fusion(f32[2,16,4,2048]{3,2,1,0:T(4,128)S(1)} %pad_maximum_fusion.1, f32[]{:T(128)} %bitcast.5, f32[]{:T(128)} %bitcast.4, f32[]{:T(128)} %bitcast.3, f32[2,1,4,2048]{3,2,1,0:T(4,128)S(1)} %collective-permute-done.4, f32[1,16,4,2048]{3,2,1,0:T(4,128)S(1)} %bitcast.92, ...), kind=kLoop, calls=%fused_computation.35 | loop fusion | flops 5505024 | bytes 3866636 | tf_op jit(solution)/shard_map/mul | solution.py:36
  48.9 2.3 %multiply_subtract_fusion = f32[2,16,4,2048]{3,2,1,0:T(4,128)S(1)} fusion(f32[2,16,4,2048]{3,2,1,0:T(4,128)S(1)} %pad_maximum_fusion.1, f32[2,1,4,2048]{3,2,1,0:T(4,128)S(1)} %collective-permute-done.4, f32[1,16,4,2048]{3,2,1,0:T(4,128)S(1)} %bitcast.93, f32[1,16,4,2048]{3,2,1,0:T(4,128)S(1)} %bitcast.88, f32[2,1,4,2048]{3,2,1,0:T(4,128)S(1)} %collective-permute-done.5, ...), kind=kLoop, calls=%fused_computation.36 | loop fusion | flops 4980736 | bytes 3866624 | tf_op jit(solution)/shard_map/sub | solution.py:35
  51.2 1.0 %fusion.7 = (f32[1,16,4,2048]{3,2,1,0:T(4,128)S(1)}, f32[1,16,4,2048]{3,2,1,0:T(4,128)S(1)}) fusion(f32[2,16,4,2048]{3,2,1,0:T(4,128)S(1)} %add_multiply_fusion, f32[16,4,2048]{2,1,0:T(4,128)S(1)} %get-tuple-element.7, f32[2,16,4,2048]{3,2,1,0:T(4,128)S(1)} %multiply_subtract_fusion, f32[16,4,2048]{2,1,0:T(4,128)S(1)} %get-tuple-element.8, ...), kind=kLoop, calls=%fused_computation.53 | loop fusion | flops 1310720 | bytes 4718592 | tf_op jit(solution)/shard_map/stack | solution.py:42
  52.8 1.0 %fusion.25 = f32[128,128]{1,0:T(8,128)S(1)} fusion(f32[128,2048]{1,0:T(8,128)S(1)} %reshape.14, f32[128,2048]{1,0:T(8,128)S(1)} %copy-done), kind=kOutput, calls=%fused_computation.87 | convolution fusion | flops 402653184 | bytes 2162688 | tf_op jit(solution)/shard_map/dot_general | solution.py:54
  54.5 13.2 %all_to_all.18 = f32[8,1,2048]{2,1,0:T(1,128)S(1)} all-to-all(f32[8,1,2048]{2,1,0:T(1,128)S(1)} %reshape.17), channel_id=1, replica_groups=mesh['gy'=8,'gz'=4] {'gy'}, dimensions={0} | all-to-all | bytes 131072 | tf_op jit(solution)/shard_map/all_to_all | solution.py:58
  68.3 0.8 %reduce = f32[8,2048]{1,0:T(8,128)S(1)} reduce(f32[8,1,2048]{2,1,0:T(1,128)S(1)} %all_to_all.18, f32[]{:T(128)} %broadcast.34), dimensions={1}, to_apply=%all_to_all.13.reduce_sub_computation | reduce | bytes 131076 | tf_op jit(solution)/shard_map/all_to_all | solution.py:58
  (30 shorter events, 6.0 us)
Async XLA Ops:
  0.0 52.8 %copy-start = (f32[128,2048]{1,0:T(8,128)S(1)}, f32[128,2048]{1,0:T(8,128)}, u32[]{:S(2)}) copy-start(f32[128,2048]{1,0:T(8,128)} %param.10) | copy-start | bytes 3145732
  0.0 6.2 %copy-start.1 = (f32[16,4,2048]{2,1,0:T(4,128)S(1)}, f32[16,4,2048]{2,1,0:T(4,128)}, u32[]{:S(2)}) copy-start(f32[16,4,2048]{2,1,0:T(4,128)} %param.7) | copy-start | bytes 1572868
  0.0 6.2 %copy-start.2 = (f32[16,4,2048]{2,1,0:T(4,128)S(1)}, f32[16,4,2048]{2,1,0:T(4,128)}, u32[]{:S(2)}) copy-start(f32[16,4,2048]{2,1,0:T(4,128)} %param.6) | copy-start | bytes 1572868
  1.0 12.6 %copy-start.5 = (f32[3]{0:T(128)S(1)}, f32[3]{0:T(128)}, u32[]{:S(2)}) copy-start(f32[3]{0:T(128)} %param.9) | copy-start | bytes 40
  1.0 4.3 %collective-permute-start = (f32[2,1,4,2048]{3,2,1,0:T(4,128)S(1)}, f32[2,1,4,2048]{3,2,1,0:T(4,128)S(1)}, u32[]{:S(2)}, u32[]{:S(2)}) collective-permute-start(f32[2,1,4,2048]{3,2,1,0:T(4,128)S(1)} %get-tuple-element.16), channel_id=1, source_target_pairs={{4,0},{8,4},{12,8},{16,12},{20,16},{24,20},{28,24},{5,1},{9,5},{13... | collective-permute-start | bytes 196616 | tf_op jit(solution)/shard_map/ppermute | solution.py:19
  2.3 3.9 %collective-permute-start.1 = (f32[2,1,4,2048]{3,2,1,0:T(4,128)S(1)}, f32[2,1,4,2048]{3,2,1,0:T(4,128)S(1)}, u32[]{:S(2)}, u32[]{:S(2)}) collective-permute-start(f32[2,1,4,2048]{3,2,1,0:T(4,128)S(1)} %get-tuple-element.15), channel_id=1, source_target_pairs={{0,4},{4,8},{8,12},{12,16},{16,20},{20,24},{24,28},{1,5},{5,9},{9,... | collective-permute-start | bytes 196616 | tf_op jit(solution)/shard_map/ppermute | solution.py:17
  6.7 11.8 %collective-permute-start.2 = (f32[2,18,1,2048]{3,2,1,0:T(1,128)S(1)}, f32[2,18,1,2048]{3,2,1,0:T(1,128)S(1)}, u32[]{:S(2)}, u32[]{:S(2)}) collective-permute-start(f32[2,18,1,2048]{3,2,1,0:T(1,128)S(1)} %get-tuple-element.12), channel_id=1, source_target_pairs={{1,0},{2,1},{3,2},{5,4},{6,5},{7,6},{9,8},{10,9},{11,10},{13,12},{... | collective-permute-start | bytes 884744 | tf_op jit(solution)/shard_map/ppermute | solution.py:19
  8.0 12.3 %collective-permute-start.3 = (f32[2,18,1,2048]{3,2,1,0:T(1,128)S(1)}, f32[2,18,1,2048]{3,2,1,0:T(1,128)S(1)}, u32[]{:S(2)}, u32[]{:S(2)}) collective-permute-start(f32[2,18,1,2048]{3,2,1,0:T(1,128)S(1)} %get-tuple-element.11), channel_id=1, source_target_pairs={{0,1},{1,2},{2,3},{4,5},{5,6},{6,7},{8,9},{9,10},{10,11},{12,13},{... | collective-permute-start | bytes 884744 | tf_op jit(solution)/shard_map/ppermute | solution.py:17
  22.5 4.4 %copy-start.3 = (f32[16,4,2048]{2,1,0:T(4,128)S(1)}, f32[16,4,2048]{2,1,0:T(4,128)}, u32[]{:S(2)}) copy-start(f32[16,4,2048]{2,1,0:T(4,128)} %param.8) | copy-start | bytes 1572868
  27.9 4.7 %collective-permute-start.4 = (f32[2,1,4,2048]{3,2,1,0:T(4,128)S(1)}, f32[2,1,4,2048]{3,2,1,0:T(4,128)S(1)}, u32[]{:S(2)}, u32[]{:S(2)}) collective-permute-start(f32[2,1,4,2048]{3,2,1,0:T(4,128)S(1)} %get-tuple-element.14), channel_id=1, source_target_pairs={{4,0},{8,4},{12,8},{16,12},{20,16},{24,20},{28,24},{5,1},{9,5},{13... | collective-permute-start | bytes 196616 | tf_op jit(solution)/shard_map/ppermute | solution.py:19
  29.2 4.3 %collective-permute-start.5 = (f32[2,1,4,2048]{3,2,1,0:T(4,128)S(1)}, f32[2,1,4,2048]{3,2,1,0:T(4,128)S(1)}, u32[]{:S(2)}, u32[]{:S(2)}) collective-permute-start(f32[2,1,4,2048]{3,2,1,0:T(4,128)S(1)} %get-tuple-element.13), channel_id=1, source_target_pairs={{0,4},{4,8},{8,12},{12,16},{16,20},{20,24},{24,28},{1,5},{5,9},{9,... | collective-permute-start | bytes 196616 | tf_op jit(solution)/shard_map/ppermute | solution.py:17
  34.0 8.8 %collective-permute-start.6 = (f32[2,18,1,2048]{3,2,1,0:T(1,128)S(1)}, f32[2,18,1,2048]{3,2,1,0:T(1,128)S(1)}, u32[]{:S(2)}, u32[]{:S(2)}) collective-permute-start(f32[2,18,1,2048]{3,2,1,0:T(1,128)S(1)} %get-tuple-element.10), channel_id=1, source_target_pairs={{1,0},{2,1},{3,2},{5,4},{6,5},{7,6},{9,8},{10,9},{11,10},{13,12},{... | collective-permute-start | bytes 884744 | tf_op jit(solution)/shard_map/ppermute | solution.py:19
  35.3 9.3 %collective-permute-start.7 = (f32[2,18,1,2048]{3,2,1,0:T(1,128)S(1)}, f32[2,18,1,2048]{3,2,1,0:T(1,128)S(1)}, u32[]{:S(2)}, u32[]{:S(2)}) collective-permute-start(f32[2,18,1,2048]{3,2,1,0:T(1,128)S(1)} %get-tuple-element.9), channel_id=1, source_target_pairs={{0,1},{1,2},{2,3},{4,5},{5,6},{6,7},{8,9},{9,10},{10,11},{12,13},{... | collective-permute-start | bytes 884744 | tf_op jit(solution)/shard_map/ppermute | solution.py:17
  69.1 0.9 %copy-start.4 = (f32[128,128]{1,0:T(8,128)S(1)}, f32[128,128]{1,0:T(8,128)}, u32[]{:S(2)}) copy-start(f32[128,128]{1,0:T(8,128)} %param.11) | copy-start | bytes 196612
where the time goes:
time: 71.3 us; the launch traced here: 70.9 us
  starting transfers between devices  21.9 us (31%)
  other arithmetic  18.9 us (27%)
  blocking collectives  13.2 us (19%)
  waiting for transfers between devices  11.5 us (16%)
  local copies, waits for them, and re-layouts  3.8 us (5%)
  matrix products  1.26 us (2%)
    ppermute x4, starting transfers between devices, extended(): lax.ppermute(tail, axis, [(i, (i + 1) % count) for i in range(ends)])  16.8 us
    all_to_all x1, blocking collectives, per_device(): lax.all_to_all(projected, 'gy', split_axis=0, concat_axis=2, tiled=True)  13.2 us
    mul x2, other arithmetic, advance(): 0.5 * (velocity[0] * (east - west) + velocity[1] * (north - south) + velo...  8.69 us
    ppermute x4, waiting for transfers between devices, extended(): lax.ppermute(head, axis, [((i + 1) % count, i) for i in range(ends)])  6.24 us
    ppermute x4, waiting for transfers between devices, extended(): lax.ppermute(tail, axis, [(i, (i + 1) % count) for i in range(ends)])  5.22 us
    ppermute x4, starting transfers between devices, extended(): lax.ppermute(head, axis, [((i + 1) % count, i) for i in range(ends)])  5.17 us
    sub x2, other arithmetic, advance(): lap = east + west + north + south + upper + lower - 6.0 * core  4.58 us
    another operation x4, other arithmetic, advance(): return jnp.stack([new_fuel, new_oxid])  1.62 us
  transfers between devices with their start and end apart: 8, of which 6 were waited for; matrix products, arithmetic and copies ran while one was open for 2% of the time, Pallas kernels for 0%

commit v1 on v0

v1 whole, which is shorter than its diff:
```python
import functools

import jax
import jax.numpy as jnp
from jax import lax
from jax.experimental import pallas as pl
from jax.experimental.pallas import tpu as pltpu
from jax.sharding import PartitionSpec as P

DIFFUSION = (0.1, 0.05)
F32 = jnp.float32
BF16 = jnp.bfloat16
LANES = 128
VMEM_LIMIT = 16 * 1024 * 1024


def swaps(count, first):
    out = []
    for i in range(first, count - 1, 2):
        out += [(i, i + 1), (i + 1, i)]
    return out


def lane_view(cells):
    rows, planes, width = cells.shape
    tiles = width // LANES
    return (
        cells.reshape(rows, planes, tiles, LANES)
        .transpose(0, 2, 1, 3)
        .reshape(rows * tiles * planes, LANES)
    )


def call(body, outs, n_in, smem=(), aliases=None, scratch=(), flops=0, size=0):
    specs = [
        pl.BlockSpec(memory_space=pltpu.SMEM if i in smem else pltpu.VMEM)
        for i in range(n_in)
    ]
    return pl.pallas_call(
        body,
        out_shape=[jax.ShapeDtypeStruct(s, d) for s, d in outs],
        in_specs=specs,
        out_specs=[pl.BlockSpec(memory_space=pltpu.VMEM) for _ in outs],
        scratch_shapes=scratch,
        input_output_aliases=aliases or {},
        compiler_params=pltpu.CompilerParams(vmem_limit_bytes=VMEM_LIMIT),
        cost_estimate=pl.CostEstimate(flops=flops, bytes_accessed=size, transcendentals=0),
    )


def split(x):
    high = x.astype(BF16)
    return high, (x - high.astype(F32)).astype(BF16)


def product(a, b):
    return lax.dot_general(a, b, (((1,), (1,)), ((), ())), preferred_element_type=F32)


def project(x, s_high, s_low):
    high, low = split(x)
    return product(high, s_high) + product(low, s_high) + product(high, s_low)


def along_x(c, d, v):
    width = c.shape[1]
    lane = lax.broadcasted_iota(jnp.int32, c.shape, 1)
    east = jnp.where(lane == width - 1, 0.0, pltpu.roll(c, width - 1, 1))
    west = jnp.where(lane == 0, 0.0, pltpu.roll(c, 1, 1))
    return (1.0 - 6.0 * d) * c + (d - 0.5 * v) * east + (d + 0.5 * v) * west


def edge_planes(planes):
    odd = lax.rem(lax.axis_index("gz"), 2)
    first = jnp.where(odd == 0, planes - 1, 0)
    return first, planes - 1 - first


def faces_kernel(dims, a_ref, b_ref, za_ref, zb_ref, ya_ref, yb_ref):
    rows, planes, width = dims
    tiles = width // LANES
    pa, pb = edge_planes(planes)
    even = lax.rem(lax.axis_index("gy"), 2) == 0
    for f, ref in enumerate((a_ref, b_ref)):
        for t in range(tiles):
            cols = slice(t * LANES, (t + 1) * LANES)
            for p, out in ((pa, za_ref), (pb, zb_ref)):
                out[f * rows : (f + 1) * rows, cols] = ref[
                    pl.ds(t * planes + p, rows, stride=tiles * planes), :
                ]
            head = ref[t * planes : (t + 1) * planes, :]
            last = (rows - 1) * tiles * planes + t * planes
            tail = ref[last : last + planes, :]
            ya_ref[f * planes : (f + 1) * planes, cols] = jnp.where(even, tail, head)
            yb_ref[f * planes : (f + 1) * planes, cols] = jnp.where(even, head, tail)


def local_kernel(
    dims, a_ref, b_ref, r_ref, s_ref, v_ref, f_ref, rate_ref, c_ref, sh_ref, sl_ref, cells
):
    rows, planes, width = dims
    tiles = width // LANES
    for z in range(planes):
        for t in range(tiles):
            cols = slice(t * LANES, (t + 1) * LANES)
            take = pl.ds(t * planes + z, rows, stride=tiles * planes)
            cells[0, z, :, cols] = a_ref[take, :]
            cells[1, z, :, cols] = b_ref[take, :]
            rate_ref[z, :, cols] = r_ref[take, :]
    row = lax.broadcasted_iota(jnp.int32, (rows, width), 0)
    for z in range(planes):
        react = rate_ref[z] * cells[0, z] * cells[1, z]
        for f, d in enumerate(DIFFUSION):
            c = cells[f, z]
            new = along_x(c, d, v_ref[0])
            north = jnp.where(row == rows - 1, 0.0, pltpu.roll(c, rows - 1, 0))
            south = jnp.where(row == 0, 0.0, pltpu.roll(c, 1, 0))
            new += (d - 0.5 * v_ref[1]) * north + (d + 0.5 * v_ref[1]) * south
            if z < planes - 1:
                new += (d - 0.5 * v_ref[2]) * cells[f, z + 1]
            if z > 0:
                new += (d + 0.5 * v_ref[2]) * cells[f, z - 1]
            f_ref[f, z] = new - react if f == 0 else new + react
    s_high, s_low = split(s_ref[...])
    sh_ref[...] = s_high
    sl_ref[...] = s_low
    edges = jnp.concatenate(
        [cells[0, 0], cells[1, 0], cells[0, planes - 1], cells[1, planes - 1]], axis=0
    )
    c_ref[...] = project(edges, s_high, s_low)


def rows_kernel(dims, f_in, ya_ref, yb_ref, sh_ref, sl_ref, v_ref, f_ref, ea_ref, eb_ref):
    rows, planes, width = dims
    even = lax.rem(lax.axis_index("gy"), 2) == 0
    for f, d in enumerate(DIFFUSION):
        for z in range(planes):
            at = f * planes + z
            first, second = ya_ref[at : at + 1, :], yb_ref[at : at + 1, :]
            north = jnp.where(even, first, second)
            south = jnp.where(even, second, first)
            f_ref[f, z, rows - 1 : rows, :] = (
                f_in[f, z, rows - 1 : rows, :] + (d - 0.5 * v_ref[1]) * north
            )
            f_ref[f, z, 0:1, :] = f_in[f, z, 0:1, :] + (d + 0.5 * v_ref[1]) * south
    pa, pb = edge_planes(planes)
    edges = jnp.concatenate([f_ref[0, pa], f_ref[1, pa], f_ref[0, pb], f_ref[1, pb]], axis=0)
    e = project(edges, sh_ref[...], sl_ref[...])
    ea_ref[...] = e[: 2 * rows]
    eb_ref[...] = e[2 * rows :]


def second_step(a, b, rate, v_ref):
    react = rate * a * b
    return [
        a,
        b,
        along_x(a, DIFFUSION[0], v_ref[0]) - react,
        along_x(b, DIFFUSION[1], v_ref[0]) + react,
    ]


def inner_kernel(dims, f_ref, rate_ref, sh_ref, sl_ref, v_ref, out_ref):
    rows, planes, width = dims
    for z in range(1, planes - 1):
        block = jnp.concatenate(
            second_step(f_ref[0, z], f_ref[1, z], rate_ref[z], v_ref), axis=0
        )
        out = project(block, sh_ref[...], sl_ref[...])
        for i in range(4):
            out_ref[i, z - 1] = out[i * rows : (i + 1) * rows]


def edges_kernel(
    dims, packed, f_ref, rate_ref, za_ref, zb_ref, ea_ref, eb_ref, c_ref, in_ref,
    sh_ref, sl_ref, v_ref, out_ref, p_scr, w_scr,
):
    rows, planes, width = dims
    here, count = lax.axis_index("gz"), lax.axis_size("gz")
    pa, pb = edge_planes(planes)
    blocks = []
    for p, h_ref in ((pa, za_ref), (pb, zb_ref)):
        sign = jnp.where(p == planes - 1, -0.5, 0.5) * v_ref[2]
        a = f_ref[0, p] + (DIFFUSION[0] + sign) * h_ref[:rows, :]
        b = f_ref[1, p] + (DIFFUSION[1] + sign) * h_ref[rows:, :]
        blocks += second_step(a, b, rate_ref[p], v_ref)
    out = project(jnp.concatenate(blocks, axis=0), sh_ref[...], sl_ref[...])
    for f in range(2):
        for z in range(1, planes - 1):
            p_scr[f, z + 1] = in_ref[f, z - 1]
            w_scr[f, z] = in_ref[2 + f, z - 1]
    for i, (p, e_ref) in enumerate(((pa, ea_ref), (pb, eb_ref))):
        upper = p == planes - 1
        step = jnp.where(upper, 1, -1)
        there = here + step
        has = jnp.where(jnp.logical_and(there >= 0, there < count), 1.0, 0.0)
        sign = jnp.where(upper, 0.5, -0.5) * v_ref[2]
        base = pl.multiple_of(jnp.where(upper, 2 * rows, 0), 8)
        for f, d in enumerate(DIFFUSION):
            p_scr[f, p + 1] = out[(4 * i + f) * rows : (4 * i + f + 1) * rows]
            w_scr[f, p] = out[(4 * i + 2 + f) * rows : (4 * i + 3 + f) * rows]
            mine = c_ref[pl.ds(base + f * rows, rows), :]
            p_scr[f, p + 1 + step] = e_ref[f * rows : (f + 1) * rows, :] + (
                has * (d + sign)
            ) * mine
    done = []
    for f, d in enumerate(DIFFUSION):
        for z in range(planes):
            w = (
                w_scr[f, z]
                + (d - 0.5 * v_ref[2]) * p_scr[f, z + 2]
                + (d + 0.5 * v_ref[2]) * p_scr[f, z]
            )
            done.append((w, p_scr[f, z + 1]))
    if not packed:
        for q, pair in enumerate(done):
            out_ref[0, q], out_ref[1, q] = pair
        return
    keep = LANES // packed
    group = lax.broadcasted_iota(jnp.int32, (rows, LANES), 1) // keep
    for i in range(2):
        turned = [pltpu.roll(x[i], q * keep, 1) if q else x[i] for q, x in enumerate(done)]
        for dest in range(packed):
            block = turned[(0 - dest) % packed]
            for g in range(1, packed):
                block = jnp.where(group == g, turned[(g - dest) % packed], block)
            out_ref[dest, i * rows : (i + 1) * rows, :] = block


def sketch_kernel(dims, packed, got_ref, sy_ref, v_ref, out_ref):
    rows, planes, width = dims
    keep = LANES // packed
    total = packed * rows
    w = got_ref[:, :rows, :].reshape(total, LANES)
    p = got_ref[:, rows:, :].reshape(total, LANES)
    row = lax.broadcasted_iota(jnp.int32, (total, LANES), 0)
    north = jnp.where(row == total - 1, 0.0, pltpu.roll(p, total - 1, 0))
    south = jnp.where(row == 0, 0.0, pltpu.roll(p, 1, 0))
    me = lax.axis_index("gy")
    shift = lax.rem((packed - me) * keep, LANES)
    lane = lax.broadcasted_iota(jnp.int32, (total, LANES), 1)
    half = jnp.logical_and(lane >= 0, lane < planes * keep)
    w, north, south = (pltpu.roll(x, shift, 1) for x in (w, north, south))
    d = jnp.where(half, DIFFUSION[0], DIFFUSION[1])
    full = w + (d - 0.5 * v_ref[1]) * north + (d + 0.5 * v_ref[1]) * south
    res = lax.dot_general(
        full.T, sy_ref[...], (((1,), (1,)), ((), ())),
        precision=lax.Precision.HIGHEST, preferred_element_type=F32,
    )
    for q in range(packed):
        out_ref[pl.ds(q, keep, stride=packed), :] = res[q * keep : (q + 1) * keep]


def per_device(fuel, oxidant, rate, velocity, sketch_x, sketch_y):
    dims = rows, planes, width = fuel.shape
    kept = sketch_x.shape[0]
    groups = lax.axis_size("gy")
    count = lax.axis_size("gz")
    mine = kept // groups
    kinds = 2 * planes
    packed = groups if (kept == LANES and mine * kinds == LANES and groups == kinds) else 0
    bind = functools.partial
    a, b, r = lane_view(fuel), lane_view(oxidant), lane_view(rate)

    za, zb, ya, yb = call(
        bind(faces_kernel, dims),
        [((2 * rows, width), F32)] * 2 + [((2 * planes, width), F32)] * 2, 2,
        flops=1 << 20, size=1 << 22,
    )(a, b)
    za = lax.ppermute(za, "gz", swaps(count, 0))
    zb = lax.ppermute(zb, "gz", swaps(count, 1))
    ya = lax.ppermute(ya, "gy", swaps(groups, 0))
    yb = lax.ppermute(yb, "gy", swaps(groups, 1))

    cells = (2, planes, rows, width)
    field, rate_z, own, s_high, s_low = call(
        bind(local_kernel, dims),
        [
            (cells, F32), (cells[1:], F32), ((4 * rows, kept), F32),
            ((kept, width), BF16), ((kept, width), BF16),
        ],
        5, smem=(4,), scratch=[pltpu.VMEM(cells, F32)], flops=1 << 28, size=1 << 23,
    )(a, b, r, sketch_x, velocity)
    field, ea, eb = call(
        bind(rows_kernel, dims),
        [(cells, F32), ((2 * rows, kept), F32), ((2 * rows, kept), F32)],
        6, smem=(5,), aliases={0: 0}, flops=1 << 26, size=1 << 22,
    )(field, ya, yb, s_high, s_low, velocity)
    ea = lax.ppermute(ea, "gz", swaps(count, 0))
    eb = lax.ppermute(eb, "gz", swaps(count, 1))
    (inner,) = call(
        bind(inner_kernel, dims), [((4, planes - 2, rows, kept), F32)],
        5, smem=(4,), flops=1 << 27, size=1 << 22,
    )(field, rate_z, s_high, s_low, velocity)
    shape = (packed, 2 * rows, LANES) if packed else (2, kinds, rows, kept)
    (parts,) = call(
        bind(edges_kernel, dims, packed), [(shape, F32)],
        11, smem=(10,),
        scratch=[
            pltpu.VMEM((2, planes + 2, rows, kept), F32),
            pltpu.VMEM((2, planes, rows, kept), F32),
        ],
        flops=1 << 27, size=1 << 22,
    )(field, rate_z, za, zb, ea, eb, own, inner, s_high, s_low, velocity)
    if packed:
        got = lax.all_to_all(parts, "gy", split_axis=0, concat_axis=0, tiled=True)
        (out,) = call(
            bind(sketch_kernel, dims, packed), [((kept, sketch_y.shape[0]), F32)],
            3, smem=(2,), flops=1 << 24, size=1 << 19,
        )(got, sketch_y, velocity)
        return out.reshape(mine, 2, planes, sketch_y.shape[0])
    got = lax.all_to_all(parts, "gy", split_axis=3, concat_axis=2, tiled=True)
    got = got.reshape(2, 2, planes, groups * rows, mine)
    d = jnp.array(DIFFUSION, F32).reshape(2, 1, 1, 1)
    north = jnp.pad(got[1][:, :, 1:], ((0, 0), (0, 0), (0, 1), (0, 0)))
    south = jnp.pad(got[1][:, :, :-1], ((0, 0), (0, 0), (1, 0), (0, 0)))
    full = got[0] + (d - 0.5 * velocity[1]) * north + (d + 0.5 * velocity[1]) * south
    return jnp.einsum("fzyk,jy->kfzj", full, sketch_y, precision=lax.Precision.HIGHEST)


def solution(mesh):
    in_specs = (P("gy", "gz", None), P("gy", "gz", None), P("gy", "gz", None), P(), P(), P())
    out_specs = P("gy", None, "gz", None)
    return jax.shard_map(
        per_device, mesh=mesh, in_specs=in_specs, out_specs=out_specs, check_vma=False
    )
```

time: 71.3 us -> 33.3 us (0.47)
  other arithmetic: 18.9 us -> 0 us
  starting transfers between devices: 21.9 us -> 9.61 us
  waiting for transfers between devices: 11.5 us -> 0.02 us
  Pallas kernels: 0 us -> 8.74 us
  blocking collectives: 13.2 us -> 11.1 us
  matrix products: 1.26 us -> 0 us
    ppermute x8 -> x6, starting transfers between devices: 21.9 us -> 9.61 us  [the longest x1 4.44 us: per_device(): ea = lax.ppermute(ea, 'gz', swaps(count, 0))]
    ppermute x8 -> x6, waiting for transfers between devices: 11.5 us -> 0.02 us  [the longest x1 0.01 us: per_device(): ya = lax.ppermute(ya, 'gy', swaps(groups, 0))]
    pallas_call x0 -> x6, Pallas kernels: none -> 8.74 us  [the longest x1 2.36 us: per_device(): call(bind(local_kernel, dims), [(cells, F32), (cells[1:], F32), ((4 * row...]
    mul x2 -> x0, other arithmetic: 8.69 us -> none  [advance(): 0.5 * (velocity[0] * (east - west) + velocity[1] * (north - south) + velo...]
    sub x3 -> x0, other arithmetic: 5.54 us -> none  [the longest x2 4.58 us: advance(): lap = east + west + north + south + upper + lower - 6.0 * core]
    another operation x6 -> x0, other arithmetic: 2.98 us -> none  [the longest x4 1.62 us: advance(): return jnp.stack([new_fuel, new_oxid])]
    unnamed x14 -> x12, local copies, waits for them, and re-layouts: 0.84 us -> 3.14 us
    all_to_all x1, blocking collectives: 13.2 us -> 11.1 us  [per_device(): got = lax.all_to_all(parts, 'gy', split_axis=0, concat_axis=0, tiled=True)]
  transfers between devices with their start and end apart: 8 -> 6, of which waited for: 6 -> 0; matrix products, arithmetic and copies ran while one was open for 2% -> 0% of each run, Pallas kernels for 0% -> 16%
where the time goes in v1:
time: 33.3 us; the launch traced here: 32.8 us
  blocking collectives  11.1 us (33%)
  starting transfers between devices  9.61 us (29%)
  Pallas kernels  8.74 us (26%)
  local copies, waits for them, and re-layouts  3.14 us (9%)
    all_to_all x1, blocking collectives, per_device(): got = lax.all_to_all(parts, 'gy', split_axis=0, concat_axis=0, tiled=True)  11.1 us
    ppermute x1, starting transfers between devices, per_device(): ea = lax.ppermute(ea, 'gz', swaps(count, 0))  4.44 us
    unnamed x12, local copies, waits for them, and re-layouts  3.14 us
    ppermute x1, starting transfers between devices, per_device(): za = lax.ppermute(za, 'gz', swaps(count, 0))  3.12 us
    pallas_call x1, Pallas kernels, per_device(): call(bind(local_kernel, dims), [(cells, F32), (cells[1:], F32), ((4 * row...  2.36 us
    pallas_call x1, Pallas kernels, per_device(): call(bind(inner_kernel, dims), [((4, planes - 2, rows, kept), F32)], 5, s...  1.76 us
    pallas_call x1, Pallas kernels, per_device(): call(bind(sketch_kernel, dims, packed), [((kept, sketch_y.shape[0]), F32)...  1.55 us
    pallas_call x1, Pallas kernels, per_device(): call(bind(edges_kernel, dims, packed), [(shape, F32)], 11, smem=(10,), sc...  1.49 us
  transfers between devices with their start and end apart: 6, of which 0 were waited for; matrix products, arithmetic and copies ran while one was open for 0% of the time, Pallas kernels for 16%

profile of v1, /device:TPU:0, one launch (start us, length us, event | category | flops | bytes accessed | tf_op | source)
XLA Modules:
  0.0 32.8 jit_solution(11380206854857969685)
XLA Ops:
  0.0 1.0 %copy-done = f32[16,4,2048]{2,1,0:T(4,128)S(1)} copy-done((f32[16,4,2048]{2,1,0:T(4,128)S(1)}, f32[16,4,2048]{2,1,0:T(4,128)}, u32[]{:S(2)}) %copy-start) | copy-done | bytes 524312
  1.0 1.0 %copy-done.1 = f32[16,4,2048]{2,1,0:T(4,128)S(1)} copy-done((f32[16,4,2048]{2,1,0:T(4,128)S(1)}, f32[16,4,2048]{2,1,0:T(4,128)}, u32[]{:S(2)}) %copy-start.1) | copy-done | bytes 524312
  2.1 0.3 %shard_map.65 = (f32[32,2048]{1,0:T(8,128)S(1)}, f32[32,2048]{1,0:T(8,128)S(1)}, f32[8,2048]{1,0:T(8,128)S(1)}, f32[8,2048]{1,0:T(8,128)S(1)}) custom-call(f32[1024,128]{1,0:T(8,128)S(1)} %bitcast.16, f32[1024,128]{1,0:T(8,128)S(1)} %bitcast.18), custom_call_target="tpu_custom_call" | custom-call | flops 1048576 | bytes 4194304 | tf_op jit(solution)/shard_map/pallas_call | solution.py:265
  2.4 3.1 %collective-permute-start.2 = (f32[32,2048]{1,0:T(8,128)S(1)}, f32[32,2048]{1,0:T(8,128)S(1)}, u32[]{:S(2)}, u32[]{:S(2)}) collective-permute-start(f32[32,2048]{1,0:T(8,128)S(1)} %get-tuple-element.24), channel_id=1, source_target_pairs={{0,1},{1,0},{2,3},{3,2},{4,5},{5,4},{6,7},{7,6},{8,9},{9,8},{10,11... | collective-permute-start | bytes 786440 | tf_op jit(solution)/shard_map/ppermute | solution.py:270
  5.5 0.7 %collective-permute-start.3 = (f32[32,2048]{1,0:T(8,128)S(1)}, f32[32,2048]{1,0:T(8,128)S(1)}, u32[]{:S(2)}, u32[]{:S(2)}) collective-permute-start(f32[32,2048]{1,0:T(8,128)S(1)} %get-tuple-element.25), channel_id=1, source_target_pairs={{1,2},{2,1},{5,6},{6,5},{9,10},{10,9},{13,14},{14,13},{17,18},{18,... | collective-permute-start | bytes 786440 | tf_op jit(solution)/shard_map/ppermute | solution.py:271
  6.2 0.1 collective-permute-start
  6.3 0.0 copy-start.5
  6.3 0.7 %collective-permute-start.1 = (f32[8,2048]{1,0:T(8,128)S(1)}, f32[8,2048]{1,0:T(8,128)S(1)}, u32[]{:S(2)}, u32[]{:S(2)}) collective-permute-start(f32[8,2048]{1,0:T(8,128)S(1)} %get-tuple-element.19), channel_id=1, source_target_pairs={{4,8},{8,4},{12,16},{16,12},{20,24},{24,20},{5,9},{9,5},{13,17},{1... | collective-permute-start | bytes 196616 | tf_op jit(solution)/shard_map/ppermute | solution.py:273
  7.0 0.0 copy-start.3
  7.0 1.0 %copy-done.3 = f32[16,4,2048]{2,1,0:T(4,128)S(1)} copy-done((f32[16,4,2048]{2,1,0:T(4,128)S(1)}, f32[16,4,2048]{2,1,0:T(4,128)}, u32[]{:S(2)}) %copy-start.3) | copy-done | bytes 524312
  8.0 2.4 %shard_map.64 = (f32[2,4,16,2048]{3,2,1,0:T(8,128)S(1)}, f32[4,16,2048]{2,1,0:T(8,128)S(1)}, f32[64,128]{1,0:T(8,128)S(1)}, bf16[128,2048]{1,0:T(8,128)(2,1)S(1)}, bf16[128,2048]{1,0:T(8,128)(2,1)S(1)}) custom-call(f32[1024,128]{1,0:T(8,128)S(1)} %bitcast.17, f32[1024,128]{1,0:T(8,128)S(1)} %bitcast.19, f32[1024,128]{1,0:T(8,128)S(1)} %bitcast.20, ...), custom_call_target="tpu_custom_call" | custom-call | flops 268435456 | bytes 8388608 | tf_op jit(solution)/shard_map/pallas_call | solution.py:276
  10.4 0.0 collective-permute-done.ya_ref
  10.4 0.0 collective-permute-done.1.yb_ref
  10.4 1.2 %shard_map.66 = (f32[2,4,16,2048]{3,2,1,0:T(8,128)S(1)}, f32[32,128]{1,0:T(8,128)S(1)}, f32[32,128]{1,0:T(8,128)S(1)}) custom-call(f32[2,4,16,2048]{3,2,1,0:T(8,128)S(1)} %get-tuple-element.17.f_in, f32[8,2048]{1,0:T(8,128)S(1)} %collective-permute-done.ya_ref, f32[8,2048]{1,0:T(8,128)S(1)} %collective-permute-done.1.yb_ref, ...), custom_call_target="tpu_custom_call", output_to_operand_aliasing={{0}: (0, {})} | custom-call | flops 67108864 | bytes 4194304 | tf_op jit(solution)/shard_map/pallas_call | solution.py:284
  11.7 4.4 %collective-permute-start.4 = (f32[32,128]{1,0:T(8,128)S(1)}, f32[32,128]{1,0:T(8,128)S(1)}, u32[]{:S(2)}, u32[]{:S(2)}) collective-permute-start(f32[32,128]{1,0:T(8,128)S(1)} %get-tuple-element.26), channel_id=1, source_target_pairs={{0,1},{1,0},{2,3},{3,2},{4,5},{5,4},{6,7},{7,6},{8,9},{9,8},{10,11... | collective-permute-start | bytes 49160 | tf_op jit(solution)/shard_map/ppermute | solution.py:289
  16.1 0.7 %collective-permute-start.5 = (f32[32,128]{1,0:T(8,128)S(1)}, f32[32,128]{1,0:T(8,128)S(1)}, u32[]{:S(2)}, u32[]{:S(2)}) collective-permute-start(f32[32,128]{1,0:T(8,128)S(1)} %get-tuple-element.27), channel_id=1, source_target_pairs={{1,2},{2,1},{5,6},{6,5},{9,10},{10,9},{13,14},{14,13},{17,18},{18,... | collective-permute-start | bytes 49160 | tf_op jit(solution)/shard_map/ppermute | solution.py:290
  16.8 1.8 %shard_map.67.in_ref = f32[4,2,16,128]{3,2,1,0:T(8,128)S(1)} custom-call(f32[2,4,16,2048]{3,2,1,0:T(8,128)S(1)} %get-tuple-element.22.f_ref, f32[4,16,2048]{2,1,0:T(8,128)S(1)} %get-tuple-element.23.rate_ref, bf16[128,2048]{1,0:T(8,128)(2,1)S(1)} %get-tuple-element.20.sh_ref, bf16[128,2048]{1,0:T(8,128)(2,1)S(1)} %get-tuple-element.21.sl_ref, f32[3]{0:T(128)S(1)} %copy-done.5), custom_call_target="tpu_custom_call" | custom-call | flops 134217728 | bytes 4194304 | tf_op jit(solution)/shard_map/pallas_call | solution.py:291
  18.6 0.0 collective-permute-done.4.ea_ref
  18.6 0.0 collective-permute-done.5.eb_ref
  18.6 0.0 collective-permute-done.2.za_ref
  18.6 1.5 %shard_map.68 = f32[8,32,128]{2,1,0:T(8,128)S(1)} custom-call(f32[2,4,16,2048]{3,2,1,0:T(8,128)S(1)} %get-tuple-element.22.f_ref, f32[4,16,2048]{2,1,0:T(8,128)S(1)} %get-tuple-element.23.rate_ref, f32[32,2048]{1,0:T(8,128)S(1)} %collective-permute-done.2.za_ref, f32[32,2048]{1,0:T(8,128)S(1)} %collective-permute-done.3.zb_ref, ...), custom_call_target="tpu_custom_call" | custom-call | flops 134217728 | bytes 4194304 | tf_op jit(solution)/shard_map/pallas_call | solution.py:296
  20.1 0.0 copy-start.4
  20.1 11.1 %all_to_all.5.got_ref = f32[8,32,128]{2,1,0:T(8,128)S(1)} all-to-all(f32[8,32,128]{2,1,0:T(8,128)S(1)} %shard_map.68), channel_id=1, replica_groups=mesh['gy'=8,'gz'=4] {'gy'}, dimensions={0} | all-to-all | bytes 262144 | tf_op jit(solution)/shard_map/all_to_all | solution.py:306
  31.3 1.5 %shard_map.69 = f32[128,128]{1,0:T(8,128)} custom-call(f32[8,32,128]{2,1,0:T(8,128)S(1)} %all_to_all.5.got_ref, f32[128,128]{1,0:T(8,128)S(1)} %copy-done.4, f32[3]{0:T(128)S(1)} %copy-done.5), custom_call_target="tpu_custom_call" | custom-call | flops 16777216 | bytes 524288 | tf_op jit(solution)/shard_map/pallas_call | solution.py:307
  (7 shorter events, 0.0 us)
Async XLA Ops:
  0.0 1.0 %copy-start = (f32[16,4,2048]{2,1,0:T(4,128)S(1)}, f32[16,4,2048]{2,1,0:T(4,128)}, u32[]{:S(2)}) copy-start(f32[16,4,2048]{2,1,0:T(4,128)} %param.6) | copy-start | bytes 1572868
  1.0 1.0 %copy-start.1 = (f32[16,4,2048]{2,1,0:T(4,128)S(1)}, f32[16,4,2048]{2,1,0:T(4,128)}, u32[]{:S(2)}) copy-start(f32[16,4,2048]{2,1,0:T(4,128)} %param.7) | copy-start | bytes 1572868
  2.1 4.9 %copy-start.2 = (f32[128,2048]{1,0:T(8,128)S(1)}, f32[128,2048]{1,0:T(8,128)}, u32[]{:S(2)}) copy-start(f32[128,2048]{1,0:T(8,128)} %s_ref.1) | copy-start | bytes 3145732
  2.4 16.2 %collective-permute-start.2 = (f32[32,2048]{1,0:T(8,128)S(1)}, f32[32,2048]{1,0:T(8,128)S(1)}, u32[]{:S(2)}, u32[]{:S(2)}) collective-permute-start(f32[32,2048]{1,0:T(8,128)S(1)} %get-tuple-element.24), channel_id=1, source_target_pairs={{0,1},{1,0},{2,3},{3,2},{4,5},{5,4},{6,7},{7,6},{8,9},{9,8},{10,11... | collective-permute-start | bytes 786440 | tf_op jit(solution)/shard_map/ppermute | solution.py:270
  5.5 13.0 %collective-permute-start.3 = (f32[32,2048]{1,0:T(8,128)S(1)}, f32[32,2048]{1,0:T(8,128)S(1)}, u32[]{:S(2)}, u32[]{:S(2)}) collective-permute-start(f32[32,2048]{1,0:T(8,128)S(1)} %get-tuple-element.25), channel_id=1, source_target_pairs={{1,2},{2,1},{5,6},{6,5},{9,10},{10,9},{13,14},{14,13},{17,18},{18,... | collective-permute-start | bytes 786440 | tf_op jit(solution)/shard_map/ppermute | solution.py:271
  6.2 4.2 %collective-permute-start = (f32[8,2048]{1,0:T(8,128)S(1)}, f32[8,2048]{1,0:T(8,128)S(1)}, u32[]{:S(2)}, u32[]{:S(2)}) collective-permute-start(f32[8,2048]{1,0:T(8,128)S(1)} %get-tuple-element.18), channel_id=1, source_target_pairs={{0,4},{4,0},{8,12},{12,8},{16,20},{20,16},{24,28},{28,24},{1,5},{5... | collective-permute-start | bytes 196616 | tf_op jit(solution)/shard_map/ppermute | solution.py:272
  6.3 0.7 %copy-start.5 = (f32[3]{0:T(128)S(1)}, f32[3]{0:T(128)}, u32[]{:S(2)}) copy-start(f32[3]{0:T(128)} %v_ref.9) | copy-start | bytes 40
  6.3 4.1 %collective-permute-start.1 = (f32[8,2048]{1,0:T(8,128)S(1)}, f32[8,2048]{1,0:T(8,128)S(1)}, u32[]{:S(2)}, u32[]{:S(2)}) collective-permute-start(f32[8,2048]{1,0:T(8,128)S(1)} %get-tuple-element.19), channel_id=1, source_target_pairs={{4,8},{8,4},{12,16},{16,12},{20,24},{24,20},{5,9},{9,5},{13,17},{1... | collective-permute-start | bytes 196616 | tf_op jit(solution)/shard_map/ppermute | solution.py:273
  7.0 1.0 %copy-start.3 = (f32[16,4,2048]{2,1,0:T(4,128)S(1)}, f32[16,4,2048]{2,1,0:T(4,128)}, u32[]{:S(2)}) copy-start(f32[16,4,2048]{2,1,0:T(4,128)} %param.8) | copy-start | bytes 1572868
  11.7 6.9 %collective-permute-start.4 = (f32[32,128]{1,0:T(8,128)S(1)}, f32[32,128]{1,0:T(8,128)S(1)}, u32[]{:S(2)}, u32[]{:S(2)}) collective-permute-start(f32[32,128]{1,0:T(8,128)S(1)} %get-tuple-element.26), channel_id=1, source_target_pairs={{0,1},{1,0},{2,3},{3,2},{4,5},{5,4},{6,7},{7,6},{8,9},{9,8},{10,11... | collective-permute-start | bytes 49160 | tf_op jit(solution)/shard_map/ppermute | solution.py:289
  16.1 2.4 %collective-permute-start.5 = (f32[32,128]{1,0:T(8,128)S(1)}, f32[32,128]{1,0:T(8,128)S(1)}, u32[]{:S(2)}, u32[]{:S(2)}) collective-permute-start(f32[32,128]{1,0:T(8,128)S(1)} %get-tuple-element.27), channel_id=1, source_target_pairs={{1,2},{2,1},{5,6},{6,5},{9,10},{10,9},{13,14},{14,13},{17,18},{18,... | collective-permute-start | bytes 49160 | tf_op jit(solution)/shard_map/ppermute | solution.py:290
  20.1 11.2 %copy-start.4 = (f32[128,128]{1,0:T(8,128)S(1)}, f32[128,128]{1,0:T(8,128)}, u32[]{:S(2)}) copy-start(f32[128,128]{1,0:T(8,128)} %sy_ref.1) | copy-start | bytes 196612
